TPU v7x, 512 devices: a whole 4x4x16 slice. The times are simulated.
512 devices in a mesh: loop: 32 (over x, z_lo, core), grp: 16 (over z_hi, y).
Axes of the slice: x: 4, y: 4, z: 16 (z_hi: 4, z_lo: 4; z = z_hi * 4 + z_lo), core: 2. Of those that a mesh axis runs over, the one named last changes fastest.
Arguments:
- adjacency_tiles: bfloat16 [65536, 128, 128], P(('loop', 'grp')), may hold values from -0.046875 to 0.046875
- row_block: int32 [65536], P(('loop', 'grp')), may hold values from 0 to 31
- column_block: int32 [65536], P(('loop', 'grp')), may hold values from 0 to 15
- features: bfloat16 [65536, 256], P(('loop', 'grp')), may hold values from -6 to 6
- weight: bfloat16 [256, 256], replicated, may hold values from -0.375 to 0.375
- out_bias: float32 [256], replicated, may hold values from -3 to 3
Outputs:
- result: bfloat16 [65536, 256], P(('loop', 'grp'))
All inputs are finite; a program needn't handle non-finite values.
Results may differ from a plain program's by a relative error of at most 0.0046.
Values may be sent and summed in bfloat16 or wider, within the bound.
No kernel may reach another device: no remote copies, remote signals or barrier semaphores. Data moves between devices by JAX's collectives and lax.ppermute only.
A program may use at most 128 MiB of HBM per device.

v0:
```python
import jax
import jax.numpy as jnp
from jax import lax
from jax.sharding import PartitionSpec as P


def on_device(adjacency_tiles, row_block, column_block, features, weight, out_bias):
    tile_size = adjacency_tiles.shape[1]
    feat_width = features.shape[1]
    loop_count = lax.axis_size("loop")
    section_rows = lax.all_gather(features, "grp", axis=0, tiled=True)
    section_blocks = section_rows.reshape(-1, tile_size, feat_width)
    picked = jnp.take(section_blocks, column_block, axis=0)
    products = jnp.einsum(
        "tij,tjf->tif", adjacency_tiles, picked, preferred_element_type=jnp.float32
    )
    partial_value = jax.ops.segment_sum(products, row_block, num_segments=loop_count)
    summed = lax.psum_scatter(partial_value, "loop", scatter_dimension=0, tiled=True)
    aggregate = summed.reshape(tile_size, feat_width).astype(jnp.bfloat16)
    mixed = jnp.dot(aggregate, weight, preferred_element_type=jnp.float32) + out_bias
    return jax.nn.relu(mixed).astype(jnp.bfloat16)


def solution(mesh):
    in_specs = (
        P(("loop", "grp"), None, None),
        P(("loop", "grp")),
        P(("loop", "grp")),
        P(("loop", "grp"), None),
        P(),
        P(),
    )
    out_specs = P(("loop", "grp"), None)
    return jax.shard_map(
        on_device, mesh=mesh, in_specs=in_specs, out_specs=out_specs, check_vma=False
    )
```

profile of v0, /device:TPU:24, one launch (start us, length us, event | category | flops | bytes accessed | tf_op | source)
XLA Modules:
  0.0 333.1 jit_solution(5589250887956877626)
XLA Ops:
  6.5 0.0 copy-start
  6.5 0.0 all-gather.2.cloned.1.call-start
  6.5 0.7 all-gather.2.cloned.1.call-update
  7.3 0.0 reduce-scatter.2.cloned.1.call-start
  7.3 0.7 compare_select_fusion
  8.0 0.7 compare_and_fusion
  8.6 83.3 %all-gather.2.cloned.1.call-done = bf16[2048,256]{1,0:T(8,128)(2,1)} async-done(((bf16[128,256]{1,0:T(8,128)(2,1)}), bf16[2048,256]{1,0:T(8,128)(2,1)}) %all-gather.2.cloned.1.call-update) | async-done | bytes 1048592 | tf_op jit(solution)/shard_map/all_gather | solution.py:11
  91.9 7.8 %gather_fusion = bf16[128,128,256]{2,1,0:T(8,128)(2,1)} fusion(bf16[16,128,256]{2,1,0:T(8,128)(2,1)} %bitcast.8, s32[1024]{0:T(1024)S(1)} %pad_clamp_fusion), kind=kCustom, calls=%fused_computation | custom fusion | bytes 16777728 | tf_op jit(solution)/shard_map/jit(_take)/gather | solution.py:13
  99.7 13.1 %convolution_bitcast_fusion = f32[128,128,256]{1,2,0:T(8,128)} fusion(bf16[128,128,128]{2,1,0:T(8,128)(2,1)} %param.6, bf16[128,128,256]{2,1,0:T(8,128)(2,1)} %gather_fusion, pred[128]{0:T(512)(128)(4,1)S(1)} %compare_and_fusion), kind=kOutput, calls=%fused_computation.2 | convolution fusion | flops 1077936128 | bytes 29360256 | tf_op jit(solution)/shard_map/tij,tjf->tif/dot_general | solution.py:14
  112.8 0.0 copy-start.2
  112.8 17.5 %copy.9 = f32[128,128,256]{2,1,0:T(8,128)} copy(f32[128,128,256]{1,2,0:T(8,128)} %convolution_bitcast_fusion) | data formatting | bytes 33554432 | tf_op jit(solution)/shard_map/tij,tjf->tif/dot_general | solution.py:14
  130.3 2.4 broadcast_in_dim.19
  132.7 0.0 copy-done.2
  132.7 0.0 copy-start.1
  132.7 37.6 %scatter_fusion = f32[32,128,256]{2,1,0:T(8,128)} fusion(f32[32,128,256]{2,1,0:T(8,128)} %broadcast_in_dim.19, s32[128]{0:T(128)S(1)} %copy-done.2, f32[128,128,256]{2,1,0:T(8,128)} %copy.9), kind=kCustom, calls=%fused_computation.1 | custom fusion | flops 4194304 | bytes 50332160 | tf_op jit(solution)/shard_map/scatter-add | solution.py:17
  170.3 0.0 reduce-scatter.2.cloned.1.call-update
  170.3 154.2 %reduce-scatter.2.cloned.1.call-done = f32[1,128,256]{2,1,0:T(8,128)} async-done(((f32[32,128,256]{2,1,0:T(8,128)}), f32[1,128,256]{2,1,0:T(8,128)}) %reduce-scatter.2.cloned.1.call-update) | async-done | bytes 131088 | tf_op jit(solution)/shard_map/reduce_scatter | solution.py:18
  324.5 0.0 copy-done
  324.5 0.0 copy-done.1
  324.5 1.7 fusion.4
  (1 shorter events, 0.0 us)
Async XLA Ops:
  6.5 318.0 %copy-start = (bf16[256,256]{1,0:T(8,128)(2,1)S(1)}, bf16[256,256]{1,0:T(8,128)(2,1)}, u32[]{:S(2)}) copy-start(bf16[256,256]{1,0:T(8,128)(2,1)} %param.10) | copy-start | bytes 393220
  6.5 85.4 %all-gather.2.cloned.1.call-start = ((), (), s32[]{:S(2)}) async-start(), calls=%async_computation.1 | async-start | bytes 1114112 | tf_op jit(solution)/shard_map/all_gather | solution.py:11
  7.3 317.3 %reduce-scatter.2.cloned.1.call-start = ((), (), s32[]{:S(2)}) async-start(), calls=%async_computation.2 | async-start | bytes 4325376 | tf_op jit(solution)/shard_map/reduce_scatter | solution.py:18
  112.8 19.9 %copy-start.2 = (s32[128]{0:T(128)S(1)}, s32[128]{0:T(128)}, u32[]{:S(2)}) copy-start(s32[128]{0:T(128)} %param.7) | copy-start | bytes 1540
  132.7 191.8 %copy-start.1 = (f32[256]{0:T(256)S(1)}, f32[256]{0:T(256)}, u32[]{:S(2)}) copy-start(f32[256]{0:T(256)} %param.11) | copy-start | bytes 3076
Sparse Core Ops, SparseCore 0:
  10.3 81.5 all-gather.1
  170.5 154.0 reduce-scatter.1
where the time goes:
time: 334 us; the launch traced here: 333 us
  waiting for transfers between devices  238 us (71%)
  other arithmetic  38.9 us (12%)
  local copies, waits for them, and re-layouts  27.7 us (8%)
  matrix products  14.8 us (4%)
  between operations  13.4 us (4%)
    reduce_scatter x1, waiting for transfers between devices, on_device(): lax.psum_scatter(partial_value, 'loop', scatter_dimension=0, tiled=True)  154 us
    all_gather x1, waiting for transfers between devices, on_device(): section_rows = lax.all_gather(features, 'grp', axis=0, tiled=True)  83.3 us
    scatter-add x1, other arithmetic, on_device(): jax.ops.segment_sum(products, row_block, num_segments=loop_count)  37.6 us
    dot_general x1, local copies, waits for them, and re-layouts, on_device(): jnp.einsum('tij,tjf->tif', adjacency_tiles, picked, preferred_element_typ...  17.5 us
    dot_general x1, matrix products, on_device(): jnp.einsum('tij,tjf->tif', adjacency_tiles, picked, preferred_element_typ...  13.1 us
    gather x1, local copies, waits for them, and re-layouts, on_device(): picked = jnp.take(section_blocks, column_block, axis=0)  7.78 us
  transfers between devices with their start and end apart: 2, of which 2 were waited for; matrix products, arithmetic and copies ran while one was open for 0% of the time, Pallas kernels for 0%

commit v1 on v0

--- a/solution.py
+++ b/solution.py
@@ -4,11 +4,24 @@
 from jax.sharding import PartitionSpec as P
 
 
+def list_slots_all(buf, comm_axis):
+    row_out = jnp.concatenate(
+        lax.all_to_all(
+            jnp.stack(lax.axis_size(comm_axis) * [buf], axis=0),
+            axis_name=comm_axis,
+            split_axis=0,
+            concat_axis=0,
+        ),
+        axis=0,
+    )
+    return row_out
+
+
 def on_device(adjacency_tiles, row_block, column_block, features, weight, out_bias):
     tile_size = adjacency_tiles.shape[1]
     feat_width = features.shape[1]
     loop_count = lax.axis_size("loop")
-    section_rows = lax.all_gather(features, "grp", axis=0, tiled=True)
+    section_rows = list_slots_all(features, "grp")
     section_blocks = section_rows.reshape(-1, tile_size, feat_width)
     picked = jnp.take(section_blocks, column_block, axis=0)
     products = jnp.einsum(

time: 334 us -> 320 us (0.958)
  waiting for transfers between devices: 238 us -> 205 us
  starting transfers between devices: 0.04 us -> 18 us
    all_gather x1 -> x0, waiting for transfers between devices: 83.3 us -> none  [on_device(): section_rows = lax.all_gather(features, 'grp', axis=0, tiled=True)]
    all_to_all x0 -> x1, waiting for transfers between devices: none -> 49.4 us  [list_slots_all(): lax.all_to_all(jnp.stack(lax.axis_size(comm_axis) * [buf], axis=0), axis_...]
    all_to_all x0 -> x1, starting transfers between devices: none -> 18 us  [list_slots_all(): lax.all_to_all(jnp.stack(lax.axis_size(comm_axis) * [buf], axis=0), axis_...]
where the time goes in v1:
time: 320 us; the launch traced here: 319 us
  waiting for transfers between devices  205 us (64%)
  other arithmetic  39 us (12%)
  local copies, waits for them, and re-layouts  28.4 us (9%)
  starting transfers between devices  18 us (6%)
  matrix products  14.9 us (5%)
  between operations  13.4 us (4%)
    reduce_scatter x1, waiting for transfers between devices, on_device(): lax.psum_scatter(partial_value, 'loop', scatter_dimension=0, tiled=True)  156 us
    all_to_all x1, waiting for transfers between devices, list_slots_all(): lax.all_to_all(jnp.stack(lax.axis_size(comm_axis) * [buf], axis=0), axis_...  49.4 us
    scatter-add x1, other arithmetic, on_device(): jax.ops.segment_sum(products, row_block, num_segments=loop_count)  37.7 us
    all_to_all x1, starting transfers between devices, list_slots_all(): lax.all_to_all(jnp.stack(lax.axis_size(comm_axis) * [buf], axis=0), axis_...  18 us
    dot_general x1, local copies, waits for them, and re-layouts, on_device(): jnp.einsum('tij,tjf->tif', adjacency_tiles, picked, preferred_element_typ...  17.5 us
    dot_general x1, matrix products, on_device(): jnp.einsum('tij,tjf->tif', adjacency_tiles, picked, preferred_element_typ...  13.2 us
    gather x1, local copies, waits for them, and re-layouts, on_device(): picked = jnp.take(section_blocks, column_block, axis=0)  6.56 us
  transfers between devices with their start and end apart: 2, of which 2 were waited for; matrix products, arithmetic and copies ran while one was open for 0% of the time, Pallas kernels for 0%

profile of v1, /device:TPU:24, one launch (start us, length us, event | category | flops | bytes accessed | tf_op | source)
XLA Modules:
  0.0 319.3 jit_solution(15235057991997245929)
XLA Ops:
  6.5 0.0 copy-start
  6.5 1.9 stack.2
  8.5 18.0 %all-to-all-start = ((bf16[16,128,256]{2,1,0:T(8,128)(2,1)}), bf16[16,128,256]{2,1,0:T(8,128)(2,1)S(1)}, u32[]{:S(2)}, u32[]{:S(2)}) async-start(bf16[16,128,256]{2,1,0:T(8,128)(2,1)} %stack.2), calls=%async_computation | async-start | bytes 2097152 | tf_op jit(solution)/shard_map/all_to_all | solution.py:9
  26.4 0.0 reduce-scatter.2.cloned.1.call-start
  26.5 0.7 compare_select_fusion
  27.2 0.7 compare_and_fusion
  27.8 49.4 %all-to-all-done = bf16[16,128,256]{2,1,0:T(8,128)(2,1)S(1)} async-done(((bf16[16,128,256]{2,1,0:T(8,128)(2,1)}), bf16[16,128,256]{2,1,0:T(8,128)(2,1)S(1)}, u32[]{:S(2)}, u32[]{:S(2)}) %all-to-all-start) | async-done | bytes 1048608 | tf_op jit(solution)/shard_map/all_to_all | solution.py:9
  77.2 6.6 %gather_fusion = bf16[128,128,256]{2,1,0:T(8,128)(2,1)} fusion(bf16[16,128,256]{2,1,0:T(8,128)(2,1)S(1)} %all-to-all-done, s32[1024]{0:T(1024)S(1)} %pad_clamp_fusion), kind=kCustom, calls=%fused_computation | custom fusion | bytes 16777728 | tf_op jit(solution)/shard_map/jit(_take)/gather | solution.py:26
  83.7 13.2 %convolution_bitcast_fusion = f32[128,128,256]{1,2,0:T(8,128)} fusion(bf16[128,128,128]{2,1,0:T(8,128)(2,1)} %param.6, bf16[128,128,256]{2,1,0:T(8,128)(2,1)} %gather_fusion, pred[128]{0:T(512)(128)(4,1)S(1)} %compare_and_fusion), kind=kOutput, calls=%fused_computation.2 | convolution fusion | flops 1077936128 | bytes 29360256 | tf_op jit(solution)/shard_map/tij,tjf->tif/dot_general | solution.py:27
  97.0 0.0 copy-start.2
  97.0 17.5 %copy.9 = f32[128,128,256]{2,1,0:T(8,128)} copy(f32[128,128,256]{1,2,0:T(8,128)} %convolution_bitcast_fusion) | data formatting | bytes 33554432 | tf_op jit(solution)/shard_map/tij,tjf->tif/dot_general | solution.py:27
  114.4 2.4 broadcast_in_dim.19
  116.9 0.0 copy-done.2
  116.9 0.0 copy-start.1
  116.9 37.7 %scatter_fusion = f32[32,128,256]{2,1,0:T(8,128)} fusion(f32[32,128,256]{2,1,0:T(8,128)} %broadcast_in_dim.19, s32[128]{0:T(128)S(1)} %copy-done.2, f32[128,128,256]{2,1,0:T(8,128)} %copy.9), kind=kCustom, calls=%fused_computation.1 | custom fusion | flops 4194304 | bytes 50332160 | tf_op jit(solution)/shard_map/scatter-add | solution.py:30
  154.6 0.0 reduce-scatter.2.cloned.1.call-update
  154.6 156.1 %reduce-scatter.2.cloned.1.call-done = f32[1,128,256]{2,1,0:T(8,128)} async-done(((f32[32,128,256]{2,1,0:T(8,128)}), f32[1,128,256]{2,1,0:T(8,128)}) %reduce-scatter.2.cloned.1.call-update) | async-done | bytes 131088 | tf_op jit(solution)/shard_map/reduce_scatter | solution.py:31
  310.7 0.0 copy-done
  310.7 0.0 copy-done.1
  310.7 1.7 fusion.4
  (1 shorter events, 0.0 us)
Async XLA Ops:
  6.5 304.2 %copy-start = (bf16[256,256]{1,0:T(8,128)(2,1)S(1)}, bf16[256,256]{1,0:T(8,128)(2,1)}, u32[]{:S(2)}) copy-start(bf16[256,256]{1,0:T(8,128)(2,1)} %param.10) | copy-start | bytes 393220
  8.5 68.7 %all-to-all-start = ((bf16[16,128,256]{2,1,0:T(8,128)(2,1)}), bf16[16,128,256]{2,1,0:T(8,128)(2,1)S(1)}, u32[]{:S(2)}, u32[]{:S(2)}) async-start(bf16[16,128,256]{2,1,0:T(8,128)(2,1)} %stack.2), calls=%async_computation | async-start | bytes 2097152 | tf_op jit(solution)/shard_map/all_to_all | solution.py:9
  26.4 284.3 %reduce-scatter.2.cloned.1.call-start = ((), (), s32[]{:S(2)}) async-start(), calls=%async_computation.2 | async-start | bytes 4325376 | tf_op jit(solution)/shard_map/reduce_scatter | solution.py:31
  97.0 19.9 %copy-start.2 = (s32[128]{0:T(128)S(1)}, s32[128]{0:T(128)}, u32[]{:S(2)}) copy-start(s32[128]{0:T(128)} %param.7) | copy-start | bytes 1540
  116.9 193.8 %copy-start.1 = (f32[256]{0:T(256)S(1)}, f32[256]{0:T(256)}, u32[]{:S(2)}) copy-start(f32[256]{0:T(256)} %param.11) | copy-start | bytes 3076
Sparse Core Ops, SparseCore 0:
  154.7 155.9 reduce-scatter.1
